TPU v7x, 32 devices: a whole 2x2x4 slice. The times are simulated.
32 devices in a mesh: row: 4 (over z), col: 8 (over y, x, core).
Axes of the slice: x: 2, y: 2, z: 4, core: 2. Of those that a mesh axis runs over, the one named last changes fastest.
Arguments:
- matrix: float32 [6144, 6144], P('row', 'col'), may hold values from -160 to 160, as said below
- pattern: int32 [16, 16], replicated, may hold values from 0 to 1, as said below
- row_order: int32 [16], replicated, may hold values from 0 to 15, as said below
- col_order: int32 [16], replicated, may hold values from 0 to 15, as said below
Outputs:
- factored: float32 [6144, 6144], P('row', 'col')
Inputs may be any that keep to these rules, and one draw needn't show every extreme that they name: `row_order`: a permutation of 0 to 15. `col_order`: a permutation of 0 to 15. Symmetric with ones on the diagonal; pattern[1, 0] = 1; pattern[I, J] = 1 whenever pattern[I, 0] = pattern[J, 0] = 1, and whenever pattern[I, 1] = pattern[J, 1] = 1 with I, J >= 1. `matrix`: read in natural block order the window is symmetric, and its retained lower blocks make the pivot block of supernode 0, and that of supernode 1 after the first update, positive definite.
All inputs are finite; a program needn't handle non-finite values.
Results may differ from a plain program's by a relative error of at most 0.0003.
Values sent between devices are 32-bit elements; how exact they have to be, the bound alone decides.
No kernel may reach another device: no remote copies, remote signals or barrier semaphores. Data moves between devices by JAX's collectives and lax.ppermute only.
A program may use at most 128 MiB of HBM per device.

v0:
```python
import jax
import jax.numpy as jnp
from jax import lax
from jax.sharding import PartitionSpec as P

BLOCK = 384


def spread(value, axis, root):
    mine = lax.axis_index(axis) == root
    return lax.psum(jnp.where(mine, value, jnp.zeros_like(value)), axis)


def positions(order):
    indices = jnp.arange(order.shape[0], dtype=jnp.int32)
    return jnp.sum(jnp.where(order[None, :] == indices[:, None], indices[None, :], 0), axis=1)


def look_up(table, wanted):
    indices = jnp.arange(table.shape[0], dtype=jnp.int32)
    return jnp.sum(jnp.where(indices[None, :] == wanted[:, None], table[None, :], 0), axis=1)


def expand(flags, tall, broad):
    return jnp.repeat(jnp.repeat(flags, tall, axis=0), broad, axis=1)


def body(matrix, pattern, row_order, col_order):
    local_rows, width = matrix.shape
    total = row_order.shape[0]
    blocks_here = local_rows // BLOCK
    piece_width = min(width, BLOCK)
    piece_count = width // piece_width
    row_here = lax.axis_index("row")
    col_here = lax.axis_index("col")
    row_place = positions(row_order)
    col_place = positions(col_order)
    indices = jnp.arange(total, dtype=jnp.int32)
    stored_rows = row_here * blocks_here + jnp.arange(blocks_here, dtype=jnp.int32)
    row_ids = look_up(row_order, stored_rows)
    starts = col_here * width + piece_width * jnp.arange(piece_count, dtype=jnp.int32)
    col_ids = look_up(col_order, starts // BLOCK)
    offsets = starts % BLOCK
    row_select = (row_ids[:, None] == indices[None, :]).astype(jnp.int32)
    col_select = (col_ids[:, None] == indices[None, :]).astype(jnp.int32)
    marked = jnp.dot(jnp.dot(row_select, pattern), col_select.T)
    lower = row_ids[:, None] >= col_ids[None, :]
    retain = expand((marked == 1) & lower, BLOCK, piece_width).astype(jnp.float32)
    lower_full = expand(lower, BLOCK, piece_width).astype(jnp.float32)
    current = matrix * retain
    identity = jnp.eye(BLOCK, dtype=jnp.float32)
    for supernode in range(2):
        wanted = jnp.full((1,), supernode, jnp.int32)
        center = look_up(row_place, wanted)[0]
        root_row = center // blocks_here
        center_local = center % blocks_here
        column_start = look_up(col_place, wanted)[0] * BLOCK
        in_column = look_up(pattern[:, supernode], row_ids)
        struct_rows = ((in_column == 1) & (row_ids > supernode)).astype(jnp.float32)
        used_rows = jnp.repeat(struct_rows, BLOCK)
        anchor = column_start + 0
        section = lax.dynamic_slice_in_dim(current, anchor % width, piece_width, 1)
        received = spread(section, "col", anchor // width)
        center_rows = lax.dynamic_slice_in_dim(received, center_local * BLOCK, BLOCK, 0)
        pivot_values = spread(center_rows, "row", root_row)
        factor = jnp.linalg.cholesky(pivot_values)
        inverse = jax.scipy.linalg.solve_triangular(factor, identity, lower=True)
        scaled = jnp.dot(received * used_rows[:, None], inverse.T, precision=lax.Precision.HIGHEST)
        fetched = []
        for column_piece in range(piece_count):
            holder = look_up(row_place, col_ids[column_piece : column_piece + 1])[0]
            section = lax.dynamic_slice_in_dim(
                scaled, holder % blocks_here * BLOCK + offsets[column_piece], piece_width, 0
            )
            fetched.append(spread(section, "row", holder // blocks_here))
        across = jnp.concatenate(fetched, axis=0)
        update = jnp.dot(scaled, across.T, precision=lax.Precision.HIGHEST)
        current = current - update * lower_full
        is_center = jnp.repeat(row_ids == supernode, BLOCK)
        column = jnp.where(is_center[:, None], jnp.tile(factor, (blocks_here, 1)), scaled)
        replaced = []
        for column_piece in range(piece_count):
            present = lax.dynamic_slice_in_dim(current, column_piece * piece_width, piece_width, 1)
            replaced.append(jnp.where(col_ids[column_piece] == supernode, column, present))
        current = jnp.concatenate(replaced, axis=1)
    return current * retain


def solution(mesh):
    in_specs = (P("row", "col"), P(), P(), P())
    out_specs = P("row", "col")
    return jax.shard_map(body, mesh=mesh, in_specs=in_specs, out_specs=out_specs, check_vma=False)
```

profile of v0, /device:TPU:0, one launch (start us, length us, event | category | flops | bytes accessed | tf_op | source)
XLA Modules:
  0.0 607.0 jit_solution(9962153152874555031)
XLA Ops:
  9.5 2.0 fusion.84
  14.1 6.0 copy.17
  20.2 2.9 bitcast_select_fusion.3
  23.1 2.2 copy-done
  25.2 1.7 dynamic-slice_select_fusion
  29.5 63.3 %all-reduce.10.cloned.1.call-done = f32[1536,384]{0,1:T(8,128)} async-done(((f32[1536,384]{0,1:T(8,128)}), f32[1536,384]{0,1:T(8,128)}) %all-reduce.10.cloned.1.call-update) | async-done | bytes 2359312 | tf_op jit(solution)/shard_map/psum | solution.py:11
  92.8 1.9 dynamic-slice_select_fusion.6
  103.5 30.7 %all-reduce.12.cloned.1.call-done = f32[384,384]{0,1:T(8,128)} async-done(((f32[384,384]{0,1:T(8,128)}), f32[384,384]{0,1:T(8,128)}) %all-reduce.12.cloned.1.call-update) | async-done | bytes 589840 | tf_op jit(solution)/shard_map/psum | solution.py:11
  134.2 1.3 copy.18
  136.7 11.7 %cholesky.208 = f32[128,128]{1,0:T(8,128)S(1)} custom-call(f32[128,128]{1,0:T(8,128)S(1)} %cholesky.310), custom_call_target="Cholesky" | custom-call | tf_op jit(solution)/shard_map/jit(cholesky)/cholesky | solution.py:66
  148.5 9.8 %custom-call.20 = f32[1,128,128]{1,2,0:T(8,128)S(1)} custom-call(f32[1,128,128]{2,1,0:T(8,128)S(1)} %get-tuple-element.82), custom_call_target="InvertDiagBlocksLowerTriangular" | custom-call | tf_op jit(solution)/shard_map/jit(cholesky)/cholesky | solution.py:66
  158.9 11.7 %cholesky.227 = f32[128,128]{1,0:T(8,128)S(1)} custom-call(f32[128,128]{1,0:T(8,128)S(1)} %cholesky.314), custom_call_target="Cholesky" | custom-call | tf_op jit(solution)/shard_map/jit(cholesky)/cholesky | solution.py:66
  171.9 10.1 %custom-call.21 = f32[1,128,128]{1,2,0:T(8,128)S(1)} custom-call(f32[1,128,128]{2,1,0:T(8,128)S(1)} %get-tuple-element.79), custom_call_target="InvertDiagBlocksLowerTriangular" | custom-call | tf_op jit(solution)/shard_map/jit(cholesky)/cholesky | solution.py:66
  182.5 11.7 %cholesky.246 = f32[128,128]{1,0:T(8,128)S(1)} custom-call(f32[128,128]{1,0:T(8,128)S(1)} %convolution_subtract_fusion.7), custom_call_target="Cholesky" | custom-call | tf_op jit(solution)/shard_map/jit(cholesky)/cholesky | solution.py:66
  196.8 5.6 while.4
  197.4 1.3 bitcast_dynamic-update-slice_fusion.4
  199.3 1.3 bitcast_dynamic-update-slice_fusion.4
  201.2 1.3 bitcast_dynamic-update-slice_fusion.4
  202.4 29.5 %custom-call.22 = f32[3,128,128]{1,2,0:T(8,128)S(1)} custom-call(f32[3,128,128]{2,1,0:T(8,128)S(1)} %get-tuple-element.21), custom_call_target="InvertDiagBlocksLowerTriangular" | custom-call | tf_op jit(solution)/shard_map/jit(_solve_triangular)/triangular_solve | solution.py:67
  233.8 5.7 fusion.6
  239.5 1.4 dynamic-slice_select_fusion.5
  244.1 1.3 broadcast_in_dim.166
  247.2 1.5 tile.8
  248.6 1.6 copy.24
  250.2 46.4 %all-reduce.20.cloned.1.call-done = (f32[384,384]{0,1:T(8,128)}, f32[384,384]{0,1:T(8,128)}) async-done(((f32[384,384]{0,1:T(8,128)}, f32[384,384]{0,1:T(8,128)}), (f32[384,384]{0,1:T(8,128)}, f32[384,384]{0,1:T(8,128)})) %all-reduce.20.cloned.1.call-update) | async-done | bytes 1179664 | tf_op jit(solution)/shard_map/psum | solution.py:11
  296.6 10.6 %fusion.1 = f32[1536,768]{0,1:T(8,128)S(1)} fusion(f32[1536,768]{0,1:T(8,128)} %copy-done, f32[1536,384]{0,1:T(8,128)S(1)} %fusion.6, pred[1536,2]{0,1:T(4,128)(4,1)S(1)} %bitcast.119, f32[384,384]{0,1:T(8,128)} %get-tuple-element.51, f32[384,384]{0,1:T(8,128)} %get-tuple-element.52), kind=kOutput, calls=%fused_computation.12 | convolution fusion | flops 5438472192 | bytes 12979200 | tf_op jit(solution)/shard_map/dot_general | solution.py:77
  308.3 1.4 copy-done.1
  310.5 2.6 fusion.3
  315.9 59.7 %all-reduce.14.cloned.1.call-done = f32[1536,384]{0,1:T(8,128)} async-done(((f32[1536,384]{0,1:T(8,128)}), f32[1536,384]{0,1:T(8,128)}) %all-reduce.14.cloned.1.call-update) | async-done | bytes 2359312 | tf_op jit(solution)/shard_map/psum | solution.py:11
  375.6 1.9 dynamic-slice_select_fusion.3
  378.5 38.4 %all-reduce.16.cloned.1.call-done = f32[384,384]{0,1:T(8,128)} async-done(((f32[384,384]{0,1:T(8,128)}), f32[384,384]{0,1:T(8,128)}) %all-reduce.16.cloned.1.call-update) | async-done | bytes 589840 | tf_op jit(solution)/shard_map/psum | solution.py:11
  416.9 1.3 copy.20
  419.3 11.7 %cholesky.261 = f32[128,128]{1,0:T(8,128)S(1)} custom-call(f32[128,128]{1,0:T(8,128)S(1)} %cholesky.318), custom_call_target="Cholesky" | custom-call | tf_op jit(solution)/shard_map/jit(cholesky)/cholesky | solution.py:66
  431.1 9.8 %custom-call.23 = f32[1,128,128]{1,2,0:T(8,128)S(1)} custom-call(f32[1,128,128]{2,1,0:T(8,128)S(1)} %get-tuple-element.75), custom_call_target="InvertDiagBlocksLowerTriangular" | custom-call | tf_op jit(solution)/shard_map/jit(cholesky)/cholesky | solution.py:66
  441.5 11.7 %cholesky.280 = f32[128,128]{1,0:T(8,128)S(1)} custom-call(f32[128,128]{1,0:T(8,128)S(1)} %cholesky.322), custom_call_target="Cholesky" | custom-call | tf_op jit(solution)/shard_map/jit(cholesky)/cholesky | solution.py:66
  454.5 10.0 %custom-call.24 = f32[1,128,128]{1,2,0:T(8,128)S(1)} custom-call(f32[1,128,128]{2,1,0:T(8,128)S(1)} %get-tuple-element.72), custom_call_target="InvertDiagBlocksLowerTriangular" | custom-call | tf_op jit(solution)/shard_map/jit(cholesky)/cholesky | solution.py:66
  465.0 11.7 %cholesky.299 = f32[128,128]{1,0:T(8,128)S(1)} custom-call(f32[128,128]{1,0:T(8,128)S(1)} %convolution_subtract_fusion.6), custom_call_target="Cholesky" | custom-call | tf_op jit(solution)/shard_map/jit(cholesky)/cholesky | solution.py:66
  479.3 5.6 while.5
  480.0 1.2 bitcast_dynamic-update-slice_fusion.5
  483.7 1.2 bitcast_dynamic-update-slice_fusion.5
  485.0 29.5 %custom-call.25 = f32[3,128,128]{1,2,0:T(8,128)S(1)} custom-call(f32[3,128,128]{2,1,0:T(8,128)S(1)} %get-tuple-element.22), custom_call_target="InvertDiagBlocksLowerTriangular" | custom-call | tf_op jit(solution)/shard_map/jit(_solve_triangular)/triangular_solve | solution.py:67
  516.3 5.7 fusion.4
  522.0 1.4 dynamic-slice_select_fusion.2
  525.3 1.5 copy.26
  526.9 52.2 %all-reduce.18.cloned.1.call-done = (f32[384,384]{0,1:T(8,128)}, f32[384,384]{0,1:T(8,128)}) async-done(((f32[384,384]{0,1:T(8,128)}, f32[384,384]{0,1:T(8,128)}), (f32[384,384]{0,1:T(8,128)}, f32[384,384]{0,1:T(8,128)})) %all-reduce.18.cloned.1.call-update) | async-done | bytes 1179664 | tf_op jit(solution)/shard_map/psum | solution.py:11
  579.1 10.9 %fusion = f32[1536,768]{0,1:T(8,128)S(1)} fusion(f32[1536,384]{0,1:T(8,128)} %copy-done.2, f32[1536,384]{0,1:T(8,128)} %copy-done.1, f32[1536,384]{0,1:T(8,128)S(1)} %fusion.4, pred[1536,2]{0,1:T(4,128)(4,1)S(1)} %bitcast.120, f32[384,384]{0,1:T(8,128)} %get-tuple-element.49, f32[384,384]{0,1:T(8,128)} %get-tuple-element.50), kind=kOutput, calls=%fused_computation.11 | convolution fusion | flops 5439651840 | bytes 12979200 | tf_op jit(solution)/shard_map/dot_general | solution.py:77
  591.0 2.6 bitcast_select_fusion.2
  593.7 6.0 copy.22
  (120 shorter events, 32.2 us)
Async XLA Ops:
  6.5 86.3 %all-reduce.10.cloned.1.call-start = ((), (), s32[]{:S(2)}) async-start(), calls=%async_computation | async-start | bytes 4718592 | tf_op jit(solution)/shard_map/psum | solution.py:11
  8.2 12.0 %copy-start.9 = (s32[2]{0:T(128)}, s32[2]{0:T(128)S(1)}, u32[]{:S(2)}) copy-start(s32[2]{0:T(128)S(1)} %fusion.80) | copy-start | bytes 28
  23.1 2.2 copy-start
  27.0 2.4 copy-start.7
  27.0 107.2 %all-reduce.12.cloned.1.call-start = ((), (), s32[]{:S(2)}) async-start(), calls=%async_computation.1 | async-start | bytes 1179648 | tf_op jit(solution)/shard_map/psum | solution.py:11
  94.8 201.8 %all-reduce.20.cloned.1.call-start = ((), (), s32[]{:S(2)}) async-start(), calls=%async_computation.5 | async-start | bytes 2359296 | tf_op jit(solution)/shard_map/psum | solution.py:11
  240.9 134.8 %all-reduce.14.cloned.1.call-start = ((), (), s32[]{:S(2)}) async-start(), calls=%async_computation.2 | async-start | bytes 4718592 | tf_op jit(solution)/shard_map/psum | solution.py:11
  248.6 47.9 %copy-start.5 = (pred[1,2,4,384]{3,1,2,0:T(4,128)(4,1)S(1)}, pred[1,2,4,384]{3,1,2,0:T(4,128)(4,1)}, u32[]{:S(2)}) copy-start(pred[1,2,4,384]{3,1,2,0:T(4,128)(4,1)} %copy.25) | copy-start | bytes 9220
  296.6 10.7 %copy-start.4 = (f32[48,8,4,384]{3,1,2,0:T(8,128)S(1)}, f32[48,8,4,384]{3,1,2,0:T(8,128)}, u32[]{:S(2)}) copy-start(f32[48,8,4,384]{3,1,2,0:T(8,128)} %copy.24) | copy-start | bytes 7077892
  308.3 1.4 copy-start.1
  308.3 2.2 copy-start.2
  313.1 64.8 %copy-start.10 = (f32[4]{0:T(128)S(1)}, f32[4]{0:T(128)}, u32[]{:S(2)}) copy-start(f32[4]{0:T(128)} %get-tuple-element.84) | copy-start | bytes 52
  313.1 103.8 %all-reduce.16.cloned.1.call-start = ((), (), s32[]{:S(2)}) async-start(), calls=%async_computation.3 | async-start | bytes 1179648 | tf_op jit(solution)/shard_map/psum | solution.py:11
  377.6 201.5 %all-reduce.18.cloned.1.call-start = ((), (), s32[]{:S(2)}) async-start(), calls=%async_computation.4 | async-start | bytes 2359296 | tf_op jit(solution)/shard_map/psum | solution.py:11
  522.0 2.6 copy-start.8
  525.3 53.7 %copy-start.6 = (pred[1,2,4,384]{3,1,2,0:T(4,128)(4,1)S(1)}, pred[1,2,4,384]{3,1,2,0:T(4,128)(4,1)}, u32[]{:S(2)}) copy-start(pred[1,2,4,384]{3,1,2,0:T(4,128)(4,1)} %copy.25) | copy-start | bytes 9220
  579.1 10.9 %copy-start.3 = (f32[48,8,4,384]{3,1,2,0:T(8,128)S(1)}, f32[48,8,4,384]{3,1,2,0:T(8,128)}, u32[]{:S(2)}) copy-start(f32[48,8,4,384]{3,1,2,0:T(8,128)} %copy.26) | copy-start | bytes 7077892
Sparse Core Ops, SparseCore 0:
  27.1 65.6 all-reduce.9
  95.2 38.9 all-reduce.11
  241.0 55.5 all-reduce.19
  313.2 62.3 all-reduce.13
  377.8 38.9 all-reduce.15
  523.5 55.4 all-reduce.17
where the time goes:
time: 618 us; the launch traced here: 607 us
  waiting for transfers between devices  291 us (47%)
  other arithmetic  201 us (33%)
  local copies, waits for them, and re-layouts  42.1 us (7%)
  matrix products  39.5 us (6%)
  between operations  33.4 us (5%)
    psum x6, waiting for transfers between devices, spread(): return lax.psum(jnp.where(mine, value, jnp.zeros_like(value)), axis)  291 us
    another operation x22, other arithmetic, body(): factor = jnp.linalg.cholesky(pivot_values)  114 us
    another operation x5, other arithmetic, body(): inverse = jax.scipy.linalg.solve_triangular(factor, identity, lower=True)  59.1 us
    dot_general x2, matrix products, body(): update = jnp.dot(scaled, across.T, precision=lax.Precision.HIGHEST)  21.5 us
    unnamed x29, local copies, waits for them, and re-layouts  14.3 us
  transfers between devices with their start and end apart: 6, of which 6 were waited for; matrix products, arithmetic and copies ran while one was open for 2% of the time, Pallas kernels for 0%

commit v1 on v0

--- a/solution.py
+++ b/solution.py
@@ -6,9 +6,15 @@
 BLOCK = 384
 
 
+def gather_and_add(array, name):
+    pieces = lax.all_gather(array, name, axis=0, tiled=False)
+    result = pieces.sum(axis=0)
+    return result
+
+
 def spread(value, axis, root):
     mine = lax.axis_index(axis) == root
-    return lax.psum(jnp.where(mine, value, jnp.zeros_like(value)), axis)
+    return gather_and_add(jnp.where(mine, value, jnp.zeros_like(value)), axis)
 
 
 def positions(order):

time: 618 us -> 863 us (1.40)
  waiting for transfers between devices: 291 us -> 456 us
  local copies, waits for them, and re-layouts: 42.1 us -> 104 us
  other arithmetic: 201 us -> 223 us
    all_gather x0 -> x8, waiting for transfers between devices: none -> 455 us  [gather_and_add(): pieces = lax.all_gather(array, name, axis=0, tiled=False)]
    psum x6 -> x0, waiting for transfers between devices: 291 us -> none  [spread(): return lax.psum(jnp.where(mine, value, jnp.zeros_like(value)), axis)]
    unnamed x29 -> x33, local copies, waits for them, and re-layouts: 14.3 us -> 56.8 us
    reduce_sum x0 -> x8, other arithmetic: none -> 25.5 us  [gather_and_add(): result = pieces.sum(axis=0)]
    all_gather x0 -> x6, local copies, waits for them, and re-layouts: none -> 20.4 us  [gather_and_add(): pieces = lax.all_gather(array, name, axis=0, tiled=False)]
  transfers between devices with their start and end apart: 6 -> 8, of which waited for: 6 -> 8; matrix products, arithmetic and copies ran while one was open for 2% -> 3% of each run, Pallas kernels for 0% -> 0%
where the time goes in v1:
time: 863 us; the launch traced here: 855 us
  waiting for transfers between devices  456 us (53%)
  other arithmetic  223 us (26%)
  local copies, waits for them, and re-layouts  104 us (12%)
  matrix products  39 us (5%)
  between operations  33 us (4%)
    all_gather x8, waiting for transfers between devices, gather_and_add(): pieces = lax.all_gather(array, name, axis=0, tiled=False)  455 us
    another operation x22, other arithmetic, body(): factor = jnp.linalg.cholesky(pivot_values)  114 us
    another operation x5, other arithmetic, body(): inverse = jax.scipy.linalg.solve_triangular(factor, identity, lower=True)  59.7 us
    unnamed x33, local copies, waits for them, and re-layouts  56.8 us
    reduce_sum x8, other arithmetic, gather_and_add(): result = pieces.sum(axis=0)  25.5 us
    dot_general x2, matrix products, body(): update = jnp.dot(scaled, across.T, precision=lax.Precision.HIGHEST)  21 us
    all_gather x6, local copies, waits for them, and re-layouts, gather_and_add(): pieces = lax.all_gather(array, name, axis=0, tiled=False)  20.4 us
  transfers between devices with their start and end apart: 8, of which 8 were waited for; matrix products, arithmetic and copies ran while one was open for 3% of the time, Pallas kernels for 0%

profile of v1, /device:TPU:0, one launch (start us, length us, event | category | flops | bytes accessed | tf_op | source)
XLA Modules:
  0.0 855.3 jit_solution(5664902703343524914)
XLA Ops:
  9.5 2.0 fusion.84
  14.2 6.0 copy.23
  20.3 2.9 bitcast_select_fusion.3
  23.2 2.2 copy-done
  25.4 1.8 dynamic-slice_select_fusion
  29.7 98.9 %all-gather.17.cloned.1.call-done = f32[12288,384]{0,1:T(8,128)} async-done(((f32[1536,384]{0,1:T(8,128)}), f32[12288,384]{0,1:T(8,128)}) %all-gather.17.cloned.1.call-update) | async-done | bytes 18874384 | tf_op jit(solution)/shard_map/all_gather | solution.py:10
  128.6 19.6 %copy.30 = f32[48,8,8,1536]{3,2,1,0:T(8,128)S(1)} copy(f32[48,8,8,1536]{3,1,2,0:T(8,128)} %bitcast.136) | data formatting | bytes 37748736
  148.2 4.8 bitcast_reduce_fusion.1
  164.6 41.0 %all-gather.19.cloned.1.call-done = f32[1536,384]{0,1:T(8,128)} async-done(((f32[384,384]{0,1:T(8,128)}), f32[1536,384]{0,1:T(8,128)}) %all-gather.19.cloned.1.call-update) | async-done | bytes 2359312 | tf_op jit(solution)/shard_map/all_gather | solution.py:10
  205.5 3.1 reshape.142
  210.4 11.7 %cholesky.208 = f32[128,128]{1,0:T(8,128)S(1)} custom-call(f32[128,128]{1,0:T(8,128)S(1)} %cholesky.310), custom_call_target="Cholesky" | custom-call | tf_op jit(solution)/shard_map/jit(cholesky)/cholesky | solution.py:72
  222.1 9.8 %custom-call.20 = f32[1,128,128]{1,2,0:T(8,128)S(1)} custom-call(f32[1,128,128]{2,1,0:T(8,128)S(1)} %get-tuple-element.78), custom_call_target="InvertDiagBlocksLowerTriangular" | custom-call | tf_op jit(solution)/shard_map/jit(cholesky)/cholesky | solution.py:72
  232.5 11.7 %cholesky.227 = f32[128,128]{1,0:T(8,128)S(1)} custom-call(f32[128,128]{1,0:T(8,128)S(1)} %cholesky.314), custom_call_target="Cholesky" | custom-call | tf_op jit(solution)/shard_map/jit(cholesky)/cholesky | solution.py:72
  245.6 10.0 %custom-call.21 = f32[1,128,128]{1,2,0:T(8,128)S(1)} custom-call(f32[1,128,128]{2,1,0:T(8,128)S(1)} %get-tuple-element.75), custom_call_target="InvertDiagBlocksLowerTriangular" | custom-call | tf_op jit(solution)/shard_map/jit(cholesky)/cholesky | solution.py:72
  256.1 11.7 %cholesky.246 = f32[128,128]{1,0:T(8,128)S(1)} custom-call(f32[128,128]{1,0:T(8,128)S(1)} %convolution_subtract_fusion.7), custom_call_target="Cholesky" | custom-call | tf_op jit(solution)/shard_map/jit(cholesky)/cholesky | solution.py:72
  270.4 6.1 while.4
  276.5 29.5 %custom-call.22 = f32[3,128,128]{1,2,0:T(8,128)S(1)} custom-call(f32[3,128,128]{2,1,0:T(8,128)S(1)} %get-tuple-element.21), custom_call_target="InvertDiagBlocksLowerTriangular" | custom-call | tf_op jit(solution)/shard_map/jit(_solve_triangular)/triangular_solve | solution.py:73
  307.8 5.7 fusion.6
  325.0 38.8 %all-gather.21.cloned.1.call-done = f32[1536,384]{0,1:T(8,128)} async-done(((f32[384,384]{0,1:T(8,128)}), f32[1536,384]{0,1:T(8,128)}) %all-gather.21.cloned.1.call-update) | async-done | bytes 2359312 | tf_op jit(solution)/shard_map/all_gather | solution.py:10
  363.8 3.7 reshape.143
  367.6 3.1 reduce_sum.200
  370.6 43.4 %all-gather.23.cloned.1.call-done = f32[1536,384]{0,1:T(8,128)} async-done(((f32[384,384]{0,1:T(8,128)}), f32[1536,384]{0,1:T(8,128)}) %all-gather.23.cloned.1.call-update) | async-done | bytes 2359312 | tf_op jit(solution)/shard_map/all_gather | solution.py:10
  414.0 3.5 reshape.144
  417.5 3.9 reduce_sum.202
  421.4 10.6 %fusion.1 = f32[1536,768]{0,1:T(8,128)S(1)} fusion(f32[1536,768]{0,1:T(8,128)} %copy-done, f32[1536,384]{0,1:T(8,128)S(1)} %fusion.6, pred[1536,2]{0,1:T(4,128)(4,1)} %bitcast.143, f32[384,384]{0,1:T(8,128)} %reduce_sum.202, f32[384,384]{0,1:T(8,128)S(1)} %reduce_sum.200), kind=kOutput, calls=%fused_computation.14 | convolution fusion | flops 5438472192 | bytes 12979200 | tf_op jit(solution)/shard_map/dot_general | solution.py:83
  435.3 2.6 fusion.3
  440.2 95.2 %all-gather.25.cloned.1.call-done = f32[12288,384]{0,1:T(8,128)} async-done(((f32[1536,384]{0,1:T(8,128)}), f32[12288,384]{0,1:T(8,128)}) %all-gather.25.cloned.1.call-update) | async-done | bytes 18874384 | tf_op jit(solution)/shard_map/all_gather | solution.py:10
  535.4 20.0 %copy.33 = f32[48,8,8,1536]{3,2,1,0:T(8,128)S(1)} copy(f32[48,8,8,1536]{3,1,2,0:T(8,128)} %bitcast.135) | data formatting | bytes 37748736
  555.4 4.8 bitcast_reduce_fusion
  563.3 49.4 %all-gather.27.cloned.1.call-done = f32[1536,384]{0,1:T(8,128)} async-done(((f32[384,384]{0,1:T(8,128)}), f32[1536,384]{0,1:T(8,128)}) %all-gather.27.cloned.1.call-update) | async-done | bytes 2359312 | tf_op jit(solution)/shard_map/all_gather | solution.py:10
  612.7 2.8 reshape.146
  617.2 11.7 %cholesky.261 = f32[128,128]{1,0:T(8,128)S(1)} custom-call(f32[128,128]{1,0:T(8,128)S(1)} %cholesky.318), custom_call_target="Cholesky" | custom-call | tf_op jit(solution)/shard_map/jit(cholesky)/cholesky | solution.py:72
  629.0 9.8 %custom-call.23 = f32[1,128,128]{1,2,0:T(8,128)S(1)} custom-call(f32[1,128,128]{2,1,0:T(8,128)S(1)} %get-tuple-element.71), custom_call_target="InvertDiagBlocksLowerTriangular" | custom-call | tf_op jit(solution)/shard_map/jit(cholesky)/cholesky | solution.py:72
  639.4 11.7 %cholesky.280 = f32[128,128]{1,0:T(8,128)S(1)} custom-call(f32[128,128]{1,0:T(8,128)S(1)} %cholesky.322), custom_call_target="Cholesky" | custom-call | tf_op jit(solution)/shard_map/jit(cholesky)/cholesky | solution.py:72
  652.5 10.2 %custom-call.24 = f32[1,128,128]{1,2,0:T(8,128)S(1)} custom-call(f32[1,128,128]{2,1,0:T(8,128)S(1)} %get-tuple-element.68), custom_call_target="InvertDiagBlocksLowerTriangular" | custom-call | tf_op jit(solution)/shard_map/jit(cholesky)/cholesky | solution.py:72
  663.2 11.7 %cholesky.299 = f32[128,128]{1,0:T(8,128)S(1)} custom-call(f32[128,128]{1,0:T(8,128)S(1)} %convolution_subtract_fusion.6), custom_call_target="Cholesky" | custom-call | tf_op jit(solution)/shard_map/jit(cholesky)/cholesky | solution.py:72
  677.6 6.1 while.5
  683.8 29.5 %custom-call.25 = f32[3,128,128]{1,2,0:T(8,128)S(1)} custom-call(f32[3,128,128]{2,1,0:T(8,128)S(1)} %get-tuple-element.22), custom_call_target="InvertDiagBlocksLowerTriangular" | custom-call | tf_op jit(solution)/shard_map/jit(_solve_triangular)/triangular_solve | solution.py:73
  715.1 5.7 fusion.4
  726.6 44.6 %all-gather.29.cloned.1.call-done = f32[1536,384]{0,1:T(8,128)} async-done(((f32[384,384]{0,1:T(8,128)}), f32[1536,384]{0,1:T(8,128)}) %all-gather.29.cloned.1.call-update) | async-done | bytes 2359312 | tf_op jit(solution)/shard_map/all_gather | solution.py:10
  771.1 3.7 reshape.147
  774.8 3.1 reduce_sum.206
  777.9 43.6 %all-gather.31.cloned.1.call-done = f32[1536,384]{0,1:T(8,128)} async-done(((f32[384,384]{0,1:T(8,128)}), f32[1536,384]{0,1:T(8,128)}) %all-gather.31.cloned.1.call-update) | async-done | bytes 2359312 | tf_op jit(solution)/shard_map/all_gather | solution.py:10
  821.5 3.5 reshape.148
  825.0 3.1 reduce_sum.207
  828.1 10.4 %fusion = f32[1536,768]{0,1:T(8,128)S(1)} fusion(f32[1536,384]{0,1:T(8,128)} %copy-done.2, f32[1536,384]{0,1:T(8,128)} %copy-done.1, f32[1536,384]{0,1:T(8,128)S(1)} %fusion.4, pred[1536,2]{0,1:T(4,128)(4,1)} %bitcast.144, f32[384,384]{0,1:T(8,128)S(1)} %reduce_sum.207, f32[384,384]{0,1:T(8,128)S(1)} %reduce_sum.206), kind=kOutput, calls=%fused_computation.13 | convolution fusion | flops 5439651840 | bytes 12979200 | tf_op jit(solution)/shard_map/dot_general | solution.py:83
  839.6 2.6 bitcast_select_fusion.2
  842.2 6.0 copy.28
  (144 shorter events, 57.2 us)
Async XLA Ops:
  6.5 122.1 %all-gather.17.cloned.1.call-start = ((), (), s32[]{:S(2)}) async-start(), calls=%async_computation | async-start | bytes 21233664 | tf_op jit(solution)/shard_map/all_gather | solution.py:10
  8.2 12.1 %copy-start.9 = (s32[2]{0:T(128)}, s32[2]{0:T(128)S(1)}, u32[]{:S(2)}) copy-start(s32[2]{0:T(128)S(1)} %fusion.80) | copy-start | bytes 28
  23.2 2.2 copy-start
  27.1 178.4 %all-gather.19.cloned.1.call-start = ((), (), s32[]{:S(2)}) async-start(), calls=%async_computation.1 | async-start | bytes 2949120 | tf_op jit(solution)/shard_map/all_gather | solution.py:10
  148.2 14.1 %copy-start.7 = (s32[16,16]{1,0:T(8,128)S(1)}, s32[16,16]{1,0:T(8,128)}, u32[]{:S(2)}) copy-start(s32[16,16]{1,0:T(8,128)} %param.8) | copy-start | bytes 3076
  153.0 1.4 copy-start.3
  155.4 208.4 %all-gather.21.cloned.1.call-start = ((), (), s32[]{:S(2)}) async-start(), calls=%async_computation.2 | async-start | bytes 2949120 | tf_op jit(solution)/shard_map/all_gather | solution.py:10
  210.3 60.0 %copy-start.11 = (s32[3]{0:T(128)S(1)}, s32[3]{0:T(128)}, u32[]{:S(2)}) copy-start(s32[3]{0:T(128)} %iota_multiply_fusion) | copy-start | bytes 40
  314.9 99.1 %all-gather.23.cloned.1.call-start = ((), (), s32[]{:S(2)}) async-start(), calls=%async_computation.3 | async-start | bytes 2949120 | tf_op jit(solution)/shard_map/all_gather | solution.py:10
  315.5 219.9 %all-gather.25.cloned.1.call-start = ((), (), s32[]{:S(2)}) async-start(), calls=%async_computation.4 | async-start | bytes 21233664 | tf_op jit(solution)/shard_map/all_gather | solution.py:10
  421.4 10.6 %copy-start.6 = (f32[48,8,4,384]{3,1,2,0:T(8,128)S(1)}, f32[48,8,4,384]{3,1,2,0:T(8,128)}, u32[]{:S(2)}) copy-start(f32[48,8,4,384]{3,1,2,0:T(8,128)} %copy.31) | copy-start | bytes 7077892
  433.1 1.4 copy-start.1
  433.1 2.2 copy-start.2
  437.9 174.8 %all-gather.27.cloned.1.call-start = ((), (), s32[]{:S(2)}) async-start(), calls=%async_computation.5 | async-start | bytes 2949120 | tf_op jit(solution)/shard_map/all_gather | solution.py:10
  555.4 7.2 copy-start.10
  560.2 1.4 copy-start.4
  562.6 208.6 %all-gather.29.cloned.1.call-start = ((), (), s32[]{:S(2)}) async-start(), calls=%async_computation.6 | async-start | bytes 2949120 | tf_op jit(solution)/shard_map/all_gather | solution.py:10
  720.8 3.5 copy-start.8
  722.2 99.3 %all-gather.31.cloned.1.call-start = ((), (), s32[]{:S(2)}) async-start(), calls=%async_computation.7 | async-start | bytes 2949120 | tf_op jit(solution)/shard_map/all_gather | solution.py:10
  828.1 10.5 %copy-start.5 = (f32[48,8,4,384]{3,1,2,0:T(8,128)S(1)}, f32[48,8,4,384]{3,1,2,0:T(8,128)}, u32[]{:S(2)}) copy-start(f32[48,8,4,384]{3,1,2,0:T(8,128)} %copy.34) | copy-start | bytes 7077892
Sparse Core Ops, SparseCore 0:
  27.2 101.3 all-gather.16
  155.5 49.9 all-gather.18
  315.0 48.7 all-gather.20
  365.2 48.7 all-gather.22
  438.0 97.3 all-gather.24
  562.7 49.9 all-gather.26
  722.3 48.7 all-gather.28
  772.7 48.7 all-gather.30
